TPU v7x, 128 devices: a whole 4x4x4 slice. The times are simulated.
128 devices in a mesh: tins: 16 (over x, y_hi, core), space: 8 (over z, y_lo).
Axes of the slice: x: 4, y: 4 (y_hi: 2, y_lo: 2; y = y_hi * 2 + y_lo), z: 4, core: 2. Of those that a mesh axis runs over, the one named last changes fastest.
Arguments:
- eigvecs: bfloat16 [16, 2, 128, 3, 4096], P('tins', None, None, None, 'space'), may hold values from -6 to 6
- momenta: int32 [1, 3], replicated, may hold values from -2 to 2, as said below
- gamma_table: int32 [2, 4], replicated, may hold values from 0 to 3, as said below
- forward: bfloat16 [16, 2, 512, 128], P('tins'), may hold values from -0.375 to 0.375
- backward: bfloat16 [16, 16, 2, 512, 512], P('tins', None, None, 'space'), may hold values from -0.1875 to 0.1875
Outputs:
- three_point: float32 [16, 1, 2, 512, 128], P('tins', None, None, 'space')
Inputs may be any that keep to these rules, and one draw needn't show every extreme that they name: `momenta`: each momentum's first component is nonzero. `gamma_table`: row 0 is a permutation of the 4 spins; row 1 holds powers of i.
All inputs are finite; a program needn't handle non-finite values.
Results may differ from a plain program's by a relative error of at most 0.0049.
Values may be sent and summed in bfloat16 or wider, within the bound.
A program may use at most 64 MiB of HBM per device.

v0:
```python
import math

import jax
import jax.numpy as jnp
from jax import lax
from jax.sharding import PartitionSpec as P

NS = 4
LS = 96


def site_phases(momenta, sites):
    coord_x = sites % LS
    coord_y = sites // LS % LS
    coord_z = sites // (LS * LS)
    turns = (
        momenta[:, 0:1] * coord_x[None, :]
        + momenta[:, 1:2] * coord_y[None, :]
        + momenta[:, 2:3] * coord_z[None, :]
    ) % LS
    angle = 2.0 * math.pi / LS * turns.astype(jnp.float32)
    return (jnp.cos(angle), -jnp.sin(angle))


def spin_tables(gamma_table):
    spins = jnp.arange(NS, dtype=jnp.int32)
    onehot = (gamma_table[0][:, None] == spins[None, :]).astype(jnp.float32)
    powers = gamma_table[1]
    cosine = (powers == 0).astype(jnp.float32) - (powers == 2).astype(jnp.float32)
    sine = (powers == 1).astype(jnp.float32) - (powers == 3).astype(jnp.float32)
    return (
        (onehot * cosine[:, None]).astype(jnp.bfloat16),
        (onehot * sine[:, None]).astype(jnp.bfloat16),
    )


def elemental_terms(vectors, momenta, site_offset, sites_total):
    site_count = vectors.shape[-1]
    sites = site_offset + jnp.arange(site_count, dtype=jnp.int32)
    phase_re, phase_im = site_phases(momenta, sites)
    vec_re = vectors[0]
    vec_im = vectors[1]
    wide_re = vec_re.astype(jnp.float32)[None]
    wide_im = vec_im.astype(jnp.float32)[None]
    wave_re = (phase_re[:, None, None, :] * wide_re - phase_im[:, None, None, :] * wide_im).astype(
        jnp.bfloat16
    )
    wave_im = (phase_re[:, None, None, :] * wide_im + phase_im[:, None, None, :] * wide_re).astype(
        jnp.bfloat16
    )

    def inner(left, right):
        return jnp.einsum("acs,mbcs->mab", left, right, preferred_element_type=jnp.float32)

    elem_re = inner(vec_re, wave_re) + inner(vec_im, wave_im)
    elem_im = inner(vec_re, wave_im) - inner(vec_im, wave_re)
    scale = 1.0 / math.sqrt(3.0 * sites_total)
    return jnp.stack([elem_re, elem_im], axis=1) * scale


def rotate_forward(fwd_split, coef_re, coef_im):

    def apply(table, block):
        return jnp.einsum("st,ktbc->ksbc", table, block, preferred_element_type=jnp.float32)

    rot_re = apply(coef_re, fwd_split[:, 0]) - apply(coef_im, fwd_split[:, 1])
    rot_im = apply(coef_im, fwd_split[:, 0]) + apply(coef_re, fwd_split[:, 1])
    return (rot_re.astype(jnp.bfloat16), rot_im.astype(jnp.bfloat16))


def spin_images(elem, fwd, coef_re, coef_im):
    batch = elem.shape[0]
    moments = elem.shape[1]
    eigen_count = elem.shape[3]
    columns = fwd.shape[-1]
    spin_count = fwd.shape[2] // eigen_count
    fwd_split = fwd.reshape(batch, 2, spin_count, eigen_count, columns)
    rot_re, rot_im = rotate_forward(fwd_split, coef_re, coef_im)

    def product(left, right):
        return jnp.einsum("kmab,ksbc->kmsac", left, right, preferred_element_type=jnp.float32)

    image_re = product(elem[:, :, 0], rot_re) - product(elem[:, :, 1], rot_im)
    image_im = product(elem[:, :, 0], rot_im) + product(elem[:, :, 1], rot_re)
    image = jnp.stack([image_re, image_im], axis=2)
    return image.reshape(batch, moments, 2, spin_count * eigen_count, columns).astype(jnp.bfloat16)


def contract_summed(back_blocks, images):

    def product(left, right):
        return jnp.einsum("kij,kmjc->mic", left, right, preferred_element_type=jnp.float32)

    out_re = product(back_blocks[:, 0], images[:, :, 0]) - product(
        back_blocks[:, 1], images[:, :, 1]
    )
    out_im = product(back_blocks[:, 0], images[:, :, 1]) + product(
        back_blocks[:, 1], images[:, :, 0]
    )
    return jnp.stack([out_re, out_im], axis=1)


def on_device(eigvecs, momenta, gamma_table, forward, backward):
    space_count = lax.axis_size("space")
    time_count = lax.axis_size("tins")
    sites_local = eigvecs.shape[-1]
    site_offset = lax.axis_index("space") * sites_local
    vectors = eigvecs[0]
    partial_elem = elemental_terms(vectors, momenta, site_offset, sites_local * space_count)
    elem_bf = lax.psum(partial_elem, "space").astype(jnp.bfloat16)
    coef_re, coef_im = spin_tables(gamma_table)
    back_rows = backward[0]
    elem_piece = lax.all_gather(elem_bf[None], "tins", axis=0, tiled=True)
    fwd_piece = lax.all_gather(forward, "tins", axis=0, tiled=True)
    images = spin_images(elem_piece, fwd_piece, coef_re, coef_im)
    summed = contract_summed(back_rows, images)[None]
    return summed * (1.0 / math.sqrt(time_count))


def solution(mesh):
    placed = (
        P("tins", None, None, None, "space"),
        P(),
        P(),
        P("tins", None, None, None),
        P("tins", None, None, "space", None),
    )
    return jax.shard_map(
        on_device,
        mesh=mesh,
        in_specs=placed,
        out_specs=P("tins", None, None, "space", None),
        check_vma=False,
    )
```

profile of v0, /device:TPU:1, one launch (start us, length us, event | category | flops | bytes accessed | tf_op | source)
XLA Modules:
  0.0 176.7 jit_solution(15080566366917500254)
XLA Ops:
  6.5 0.0 all-gather.6.cloned.1.call-start
  6.5 1.4 fusion.74
  7.9 2.0 %sine_negate_fusion = (f32[512]{0:T(512)S(1)}, f32[512]{0:T(512)S(1)}) fusion(s32[]{:T(128)} %bitcast.13, s32[]{:T(128)} %bitcast.12, s32[]{:T(128)S(6)} %mul.184, s32[]{:T(128)} %bitcast.11), kind=kLoop, calls=%fused_computation.79 | loop fusion | flops 19968 | bytes 4112 | tf_op jit(solution)/shard_map/neg | solution.py:22
  9.9 1.5 convolution_bitcast_fusion
  11.4 1.5 convolution_bitcast_fusion.2
  13.0 0.0 copy-done
  13.0 0.3 fusion.13
  13.3 0.3 fusion.11
  13.6 31.1 %all-reduce.1 = bf16[1,2,128,128]{2,3,1,0:T(8,128)(2,1)S(1)} all-reduce(f32[1,2,128,128]{2,3,1,0:T(8,128)S(1)} %maximum_multiply_fusion), channel_id=1, replica_groups=mesh['tins'=16,'space'=8] {'space'}, use_global_device_ids=true, to_apply=%region_0.1 | all-reduce | flops 32768 | bytes 196608 | tf_op jit(solution)/shard_map/psum | solution.py:110
  44.7 0.7 copy.28
  45.5 0.0 all-gather.6.cloned.1.call-update
  45.5 0.0 all-gather.4.cloned.1.call-start
  45.5 0.7 all-gather.4.cloned.1.call-update
  46.3 0.0 copy-start.1
  46.3 1.8 copy.57
  48.1 48.6 %all-gather.6.cloned.1.call-done = bf16[16,2,128,128]{3,2,1,0:T(8,128)(2,1)} async-done(((bf16[1,2,128,128]{3,2,1,0:T(8,128)(2,1)}), bf16[16,2,128,128]{3,2,1,0:T(8,128)(2,1)}) %all-gather.6.cloned.1.call-update) | async-done | bytes 1048592 | tf_op jit(solution)/shard_map/all_gather | solution.py:113
  96.7 1.3 copy.58
  98.0 56.1 %all-gather.4.cloned.1.call-done = bf16[16,2,512,128]{3,2,1,0:T(8,128)(2,1)} async-done(((bf16[1,2,512,128]{3,2,1,0:T(8,128)(2,1)}), bf16[16,2,512,128]{3,2,1,0:T(8,128)(2,1)}) %all-gather.4.cloned.1.call-update) | async-done | bytes 4194320 | tf_op jit(solution)/shard_map/all_gather | solution.py:114
  154.1 2.5 %fusion.73 = (bf16[16,1,4,128,128]{4,3,2,1,0:T(8,128)(2,1)S(1)}, bf16[16,1,4,128,128]{4,3,2,1,0:T(8,128)(2,1)S(1)}) fusion(bf16[16,2,4,128,128]{4,3,2,1,0:T(8,128)(2,1)} %bitcast.166), kind=kLoop, calls=%fused_computation.108 | loop fusion | bytes 8388608 | tf_op jit(solution)/shard_map/slice | solution.py:66
  156.6 1.8 fusion.9
  158.4 1.8 fusion.8
  160.1 2.0 %fusion.6 = bf16[16,4,128,128]{3,1,2,0:T(4,128)(2,1)S(1)} fusion(f32[4,16,128,128]{3,0,2,1:T(4,128)S(1)} %fusion.9, bf16[16,1,4,128,128]{4,3,2,1,0:T(8,128)(2,1)S(1)} %get-tuple-element.5, bf16[4]{0:T(256)(128)(2,1)S(1)} %get-tuple-element.8, s32[4]{0:T(128)S(1)} %slice_bitcast_fusion.12), kind=kOutput, calls=%fused_computation.13 | convolution fusion | flops 10485792 | bytes 8388632 | tf_op jit(solution)/shard_map/st,ktbc->ksbc/dot_general | solution.py:64
  162.2 2.0 %fusion.7 = bf16[16,4,128,128]{3,1,2,0:T(4,128)(2,1)S(1)} fusion(f32[4,16,128,128]{3,0,2,1:T(4,128)S(1)} %fusion.8, bf16[16,1,4,128,128]{4,3,2,1,0:T(8,128)(2,1)S(1)} %get-tuple-element.5, bf16[4]{0:T(256)(128)(2,1)S(1)} %get-tuple-element.7, s32[4]{0:T(128)S(1)} %slice_bitcast_fusion.12), kind=kOutput, calls=%fused_computation.14 | convolution fusion | flops 10485792 | bytes 8388632 | tf_op jit(solution)/shard_map/st,ktbc->ksbc/dot_general | solution.py:64
  164.2 0.7 fusion.1
  164.9 0.7 fusion.3
  165.6 0.7 add_convert_fusion
  166.3 0.8 subtract_convert_fusion
  167.1 0.5 convolution_bitcast_fusion.5
  167.6 0.5 convolution_bitcast_fusion.7
  168.2 0.5 fusion.15
  168.7 0.5 fusion.17
  169.2 0.6 fusion.44
  (5 shorter events, 0.0 us)
Async XLA Ops:
  6.5 6.4 %copy-start = (bf16[1,2,128,3,512]{4,2,3,1,0:T(8,128)(2,1)S(1)}, bf16[1,2,128,3,512]{4,2,3,1,0:T(8,128)(2,1)}, u32[]{:S(2)}) copy-start(bf16[1,2,128,3,512]{4,2,3,1,0:T(8,128)(2,1)} %param.5) | copy-start | bytes 2359300
  6.5 90.2 %all-gather.6.cloned.1.call-start = ((), (), s32[]{:S(2)}) async-start(), calls=%async_computation.1 | async-start | bytes 1114112 | tf_op jit(solution)/shard_map/all_gather | solution.py:113
  45.5 108.6 %all-gather.4.cloned.1.call-start = ((), (), s32[]{:S(2)}) async-start(), calls=%async_computation | async-start | bytes 4456448 | tf_op jit(solution)/shard_map/all_gather | solution.py:114
  46.3 1.8 %copy-start.1 = (s32[2,4]{1,0:T(2,128)S(1)}, s32[2,4]{1,0:T(2,128)}, u32[]{:S(2)}) copy-start(s32[2,4]{1,0:T(2,128)} %param.7) | copy-start | bytes 100
Sparse Core Ops, SparseCore 0:
  45.6 51.0 all-gather.5
  99.1 54.9 all-gather.3
where the time goes:
time: 177 us
  waiting for transfers between devices  105 us (59%)
  blocking collectives  31.1 us (18%)
  matrix products  16.2 us (9%)
  between operations  13.6 us (8%)
  local copies, waits for them, and re-layouts  7.74 us (4%)
  other arithmetic  2.64 us (1%)
    all_gather x1, waiting for transfers between devices, on_device(): fwd_piece = lax.all_gather(forward, 'tins', axis=0, tiled=True)  56.1 us
    all_gather x1, waiting for transfers between devices, on_device(): elem_piece = lax.all_gather(elem_bf[None], 'tins', axis=0, tiled=True)  48.6 us
    psum x1, blocking collectives, on_device(): elem_bf = lax.psum(partial_elem, 'space').astype(jnp.bfloat16)  31.1 us
    dot_general x4, matrix products, apply(): jnp.einsum('st,ktbc->ksbc', table, block, preferred_element_type=jnp.floa...  7.55 us
    dot_general x4, matrix products, inner(): jnp.einsum('acs,mbcs->mab', left, right, preferred_element_type=jnp.float32)  3.63 us
  transfers between devices with their start and end apart: 2, of which 2 were waited for; matrix products, arithmetic and copies ran while one was open for 2% of the time, Pallas kernels for 0%

commit v1 on v0

v1 whole, which is shorter than its diff:
```python
import functools
import math

import jax
import jax.numpy as jnp
from jax import lax
from jax.experimental import pallas as pl
from jax.experimental.pallas import tpu as pltpu
from jax.sharding import PartitionSpec as P

MESH = pl.DeviceIdType.MESH
F32 = jnp.float32
BF16 = jnp.bfloat16
NEV, NS, COLORS, LS, NSRC, NT, SPACE = 128, 4, 3, 96, 128, 16, 8
SITES_TOTAL = 4096
SITES = SITES_TOTAL // SPACE
SLICE = NEV // SPACE
ORDERS = (("z", "y", "x"), ("y", "x", "z"), ("x", "z", "y"))
UNITS = ((0, 3), (3, 3), (6, 2))


def site_phases(mom_ref, space):
    site = (space * SITES + lax.broadcasted_iota(jnp.int32, (1, SITES), 1)).astype(F32)
    line = jnp.floor((site + 0.5) * (1.0 / LS))
    coord_x = site - LS * line
    coord_z = jnp.floor((line + 0.5) * (1.0 / LS))
    coord_y = line - LS * coord_z
    m = [mom_ref[0, i].astype(F32) for i in range(3)]
    turns = m[0] * coord_x + m[1] * coord_y + m[2] * coord_z
    turns = turns - LS * jnp.floor((turns + 0.5) * (1.0 / LS))
    angle = (2.0 * math.pi / LS) * turns
    return jnp.cos(angle), -jnp.sin(angle)


def kernel(
    mom_ref, gam_ref, eig_hbm, fwd_hbm, back_hbm, out_ref,
    eig, fwd, bbuf, part, rs, wgt, img0, img1, img2, fin, finr,
    load_sem, swap_sem, rs_send, rs_recv, s1, r1, s2, r2, s3, r3, s4, r4, fin_sem,
):
    t = lax.axis_index("tins")
    space = lax.axis_index("space")
    core = lax.rem(t, 2)
    me = {
        "x": lax.div(t, 4),
        "y": lax.rem(lax.div(t, 2), 2) * 2 + lax.rem(space, 2),
        "z": lax.div(space, 2),
    }
    partner = (t + 1 - 2 * core, space)

    def step(v, d):
        return lax.rem(v + (d + 4) % 4, 4) if d % 4 else v

    def neighbour(axis, d):
        at = dict(me)
        at[axis] = step(me[axis], d)
        return (
            at["x"] * 4 + lax.div(at["y"], 2) * 2 + core,
            at["z"] * 2 + lax.rem(at["y"], 2),
        )

    loads = [
        pltpu.make_async_copy(eig_hbm, eig, load_sem.at[0]),
        pltpu.make_async_copy(fwd_hbm, fwd, load_sem.at[1]),
        pltpu.make_async_copy(back_hbm.at[:, core], bbuf.at[:, core], load_sem.at[2]),
    ]
    for load in loads:
        load.start()

    barrier = pltpu.get_barrier_semaphore()
    peers = [partner]
    peers += [(t, lax.rem(space + d, SPACE)) for d in range(1, SPACE)]
    peers += [neighbour("x", d) for d in (1, -1, 2)]
    peers += [neighbour("y", 2)]
    across = lax.rem(me["y"] + 3 + 2 * lax.rem(me["y"], 2), 4)
    peers += [(me["x"] * 4 + lax.div(across, 2) * 2 + core, me["z"] * 2 + lax.rem(across, 2))]
    for peer in peers:
        pl.semaphore_signal(barrier, inc=1, device_id=peer, device_id_type=MESH)

    phase_re, phase_im = site_phases(mom_ref, space)
    loads[0].wait()
    total = jnp.zeros((NEV, 2 * NEV), F32)
    nt = (((1,), (1,)), ((), ()))
    for color in range(COLORS):
        vec_re = eig[0, color]
        vec_im = eig[1, color]
        wide_re, wide_im = vec_re.astype(F32), vec_im.astype(F32)
        wave_re = (phase_re * wide_re - phase_im * wide_im).astype(BF16)
        wave_im = (phase_re * wide_im + phase_im * wide_re).astype(BF16)
        right = jnp.concatenate([wave_re, wave_im], axis=0)
        total += lax.dot_general(vec_re, right, nt, preferred_element_type=F32)
        right = jnp.concatenate([wave_im, -wave_re], axis=0)
        total += lax.dot_general(vec_im, right, nt, preferred_element_type=F32)
    part[...] = total.reshape(SPACE, SLICE, 2 * NEV)

    pl.semaphore_wait(barrier, len(peers))
    copies = []

    def send(src, dst, send_sem, recv_sem, device):
        copy = pltpu.make_async_remote_copy(
            src_ref=src, dst_ref=dst, send_sem=send_sem, recv_sem=recv_sem,
            device_id=device, device_id_type=MESH,
        )
        copy.start()
        copies.append(copy)
        return copy

    scatter = []
    for d in range(1, SPACE):
        to = lax.rem(space + d, SPACE)
        scatter.append(send(part.at[to], rs.at[d], rs_send.at[d], rs_recv.at[d], (t, to)))
    swap = send(
        back_hbm.at[:, 1 - core], bbuf.at[:, core], swap_sem.at[0], swap_sem.at[1], partner
    )

    loads[1].wait()
    for spin in range(NS):
        source = gam_ref[0, spin]
        power = gam_ref[1, spin]
        cosine = jnp.where(power == 0, 1.0, 0.0) - jnp.where(power == 2, 1.0, 0.0)
        sine = jnp.where(power == 1, 1.0, 0.0) - jnp.where(power == 3, 1.0, 0.0)
        fwd_re = fwd[0, source].astype(F32)
        fwd_im = fwd[1, source].astype(F32)
        rot_re = (cosine * fwd_re - sine * fwd_im).astype(BF16)
        rot_im = (sine * fwd_re + cosine * fwd_im).astype(BF16)
        at = spin * 2 * NSRC
        wgt[0:NEV, at : at + NSRC] = rot_re
        wgt[0:NEV, at + NSRC : at + 2 * NSRC] = rot_im
        wgt[NEV:, at : at + NSRC] = -rot_im
        wgt[NEV:, at + NSRC : at + 2 * NSRC] = rot_re

    elem = part[space]
    for d in range(1, SPACE):
        scatter[d - 1].wait_recv()
        elem += rs[d]
    elem = (elem * (1.0 / math.sqrt(3.0 * SITES_TOTAL))).astype(BF16)
    image = jnp.dot(elem, wgt[...], preferred_element_type=F32).astype(BF16)

    imgs = (img0, img1, img2)
    for j, (a, b, c) in enumerate(ORDERS):
        first, count = UNITS[j]
        for i in range(count):
            at = (first + i) * NSRC
            imgs[j][me[c], me[b], me[a], i] = image[:, at : at + NSRC]

    def line(j, dc, db, half=None):
        _, b, c = ORDERS[j]
        ref = imgs[j].at[step(me[c], dc), step(me[b], db)]
        return ref if half is None else ref.at[pl.ds(half * 2, 2)]

    got1 = {}
    for j, (a, b, c) in enumerate(ORDERS):
        own = imgs[j].at[me[c], me[b], me[a]]
        for i, d in enumerate((1, -1, 2)):
            got1[j, i] = send(own, own, s1.at[j, i], r1.at[j, i], neighbour(a, d))
    got2, got3, got4 = {}, {}, {}

    def pass_line(j, n, db):
        c = ORDERS[j][2]
        for i, d in enumerate((1, -1)):
            got3[j, n, i] = send(
                line(j, 0, db), line(j, 0, db), s3.at[j, n, i], r3.at[j, n, i], neighbour(c, d)
            )

    def pass_on(j, n, db, i):
        d = (1, -1)[i]
        got3[j, n, i].wait_recv()
        from_plane = line(j, -d, db)
        got4[j, n] = send(
            from_plane, from_plane, s4.at[j, n], r4.at[j, n], neighbour(ORDERS[j][2], d)
        )

    for j in range(3):
        for i in range(3):
            got1[j, i].wait_recv()
        for i, d in enumerate((1, -1)):
            got2[j, i] = send(
                line(j, 0, 0), line(j, 0, 0), s2.at[j, i], r2.at[j, i], neighbour(ORDERS[j][1], d)
            )
    for j in range(3):
        pass_line(j, 0, 0)
    for i, d in enumerate((1, -1)):
        for j in range(3):
            got2[j, i].wait_recv()
            half = line(j, 0, -d, i)
            got2[j, 2 + i] = send(
                half, half, s2.at[j, 2 + i], r2.at[j, 2 + i], neighbour(ORDERS[j][1], d)
            )
            pass_line(j, 1 + i, -d)
    for j in range(3):
        pass_on(j, 0, 0, 0)
    for j in range(3):
        got2[j, 2].wait_recv()
        got2[j, 3].wait_recv()
        pass_line(j, 3, 2)
    for j in range(3):
        pass_on(j, 1, -1, 1)
    for j in range(3):
        pass_on(j, 2, 1, 1)
    for j in range(3):
        pass_on(j, 3, 2, 0)
    for j in range(3):
        for n, i in ((0, 1), (1, 0), (2, 0), (3, 1)):
            got3[j, n, i].wait_recv()
        for n in range(4):
            got4[j, n].wait_recv()

    loads[2].wait()
    swap.wait_recv()
    acc = jnp.zeros((4 * 64, 2 * NSRC), F32)
    for k in range(NT // 2):
        x, y_hi = k // 2, k % 2
        rows = []
        for spin in range(NS):
            halves = []
            for half in range(2):
                unit = spin * 2 + half
                j = 0 if unit < 3 else (1 if unit < 6 else 2)
                tiles = []
                for s in range(SPACE):
                    at = {"x": x, "y": y_hi * 2 + s % 2, "z": s // 2}
                    a, b, c = ORDERS[j]
                    tiles.append(imgs[j][at[c], at[b], at[a], unit - UNITS[j][0]])
                halves.append(jnp.concatenate(tiles, axis=0))
            rows.append(jnp.concatenate(halves, axis=1))
        right = jnp.concatenate(rows, axis=0)
        left = bbuf[k].reshape(4 * 64, NS * NEV)
        acc += jnp.dot(left, right, preferred_element_type=F32)
    for u in range(2):
        top = acc[u * 128 : u * 128 + 64]
        low = acc[u * 128 + 64 : u * 128 + 128]
        fin[u, 0] = top[:, :NSRC] - low[:, NSRC:]
        fin[u, 1] = top[:, NSRC:] + low[:, :NSRC]
    last = send(fin.at[1 - core], finr, fin_sem.at[0], fin_sem.at[1], partner)
    last.wait_recv()
    out_ref[...] = (fin[core] + finr[...]) * (1.0 / math.sqrt(NT))
    for copy in copies:
        copy.wait_send()


def on_device(eigvecs, momenta, gamma_table, forward, backward):
    eig = eigvecs[0].transpose(0, 2, 1, 3)
    fwd = forward.reshape(2, NS, NEV, NSRC)
    back = backward.reshape(NT // 2, 2, 128, NS * NEV)
    dma = pltpu.SemaphoreType.DMA
    out = pl.pallas_call(
        kernel,
        name="three_point",
        out_shape=jax.ShapeDtypeStruct((2, 64, NSRC), F32),
        in_specs=[pl.BlockSpec(memory_space=pltpu.SMEM)] * 2
        + [pl.BlockSpec(memory_space=pl.ANY)] * 3,
        out_specs=pl.BlockSpec(memory_space=pltpu.VMEM),
        scratch_shapes=[
            pltpu.VMEM((2, COLORS, NEV, SITES), BF16),
            pltpu.VMEM((2, NS, NEV, NSRC), BF16),
            pltpu.VMEM((NT // 2, 2, 128, NS * NEV), BF16),
            pltpu.VMEM((SPACE, SLICE, 2 * NEV), F32),
            pltpu.VMEM((SPACE, SLICE, 2 * NEV), F32),
            pltpu.VMEM((2 * NEV, NS * 2 * NSRC), BF16),
            *[pltpu.VMEM((4, 4, 4, count, SLICE, NSRC), BF16) for _, count in UNITS],
            pltpu.VMEM((2, 2, 64, NSRC), F32),
            pltpu.VMEM((2, 64, NSRC), F32),
            dma((3,)), dma((2,)), dma((SPACE,)), dma((SPACE,)),
            dma((3, 3)), dma((3, 3)), dma((3, 4)), dma((3, 4)),
            dma((3, 4, 2)), dma((3, 4, 2)), dma((3, 4)), dma((3, 4)), dma((2,)),
        ],
        compiler_params=pltpu.CompilerParams(collective_id=0, has_side_effects=True),
    )(momenta, gamma_table, eig, fwd, back)
    return out[None, None]


def solution(mesh):
    placed = (
        P("tins", None, None, None, "space"),
        P(),
        P(),
        P("tins", None, None, None),
        P("tins", None, None, "space", None),
    )
    return jax.shard_map(
        on_device,
        mesh=mesh,
        in_specs=placed,
        out_specs=P("tins", None, None, "space", None),
        check_vma=False,
    )
```

time: 177 us -> 38.5 us (0.22)
  waiting for transfers between devices: 105 us -> 0 us
  Pallas kernels: 0 us -> 36.8 us
  blocking collectives: 31.1 us -> 0 us
  matrix products: 16.2 us -> 0 us
  between operations: 13.6 us -> 0.01 us
  local copies, waits for them, and re-layouts: 7.74 us -> 1.47 us
  other arithmetic: 2.64 us -> 0 us
    all_gather x2 -> x0, waiting for transfers between devices: 105 us -> none  [the longest x1 56.1 us: on_device(): fwd_piece = lax.all_gather(forward, 'tins', axis=0, tiled=True)]
    pallas_call x0 -> x1, Pallas kernels: none -> 36.8 us  [on_device(): pl.pallas_call(kernel, name='three_point', out_shape=jax.ShapeDtypeStruct...]
    psum x1 -> x0, blocking collectives: 31.1 us -> none  [on_device(): elem_bf = lax.psum(partial_elem, 'space').astype(jnp.bfloat16)]
    dot_general x16 -> x0, matrix products: 16.2 us -> none  [the longest x4 7.55 us: apply(): jnp.einsum('st,ktbc->ksbc', table, block, preferred_element_type=jnp.floa...]
    slice x2 -> x0, local copies, waits for them, and re-layouts: 3.93 us -> none  [the longest x1 2.53 us: rotate_forward(): rot_re = apply(coef_re, fwd_split[:, 0]) - apply(coef_im, fwd_split[:, 1])]
    neg x1 -> x0, other arithmetic: 1.98 us -> none  [site_phases(): return (jnp.cos(angle), -jnp.sin(angle))]
  transfers between devices with their start and end apart: 2 -> 0, of which waited for: 2 -> 0; matrix products, arithmetic and copies ran while one was open for 2% -> 0% of each run, Pallas kernels for 0% -> 0%
where the time goes in v1:
time: 38.5 us; the launch traced here: 38.3 us
  Pallas kernels  36.8 us (96%)
  local copies, waits for them, and re-layouts  1.47 us (4%)
    pallas_call x1, Pallas kernels, on_device(): pl.pallas_call(kernel, name='three_point', out_shape=jax.ShapeDtypeStruct...  36.8 us
    unnamed x1, local copies, waits for them, and re-layouts  1.47 us

profile of v1, /device:TPU:1, one launch (start us, length us, event | category | flops | bytes accessed | tf_op | source)
XLA Modules:
  0.0 38.3 jit_solution(15601320992682846456)
XLA Ops:
  0.0 36.8 %three_point.1 = f32[2,64,128]{2,1,0:T(8,128)} custom-call(s32[1,3]{1,0:T(1,128)} %mom_ref.1, s32[2,4]{1,0:T(2,128)} %gam_ref.1, bf16[2,3,128,512]{3,2,1,0:T(8,128)(2,1)} %bitcast.7, bf16[2,4,128,128]{3,2,1,0:T(8,128)(2,1)} %bitcast.8, bf16[8,2,128,512]{3,2,1,0:T(8,128)(2,1)} %bitcast.6), custom_call_target="tpu_custom_call" | custom-call | tf_op jit(solution)/shard_map/three_point/pallas_call | solution.py:245
  36.8 1.5 %copy.7 = f32[1,1,2,64,128]{4,3,2,1,0:T(8,128)} copy(f32[1,1,2,64,128]{4,3,2,1,0:T(8,128)} %bitcast.9) | data formatting | bytes 131072

commit v2 on v1

v2 whole, which is shorter than its diff:
```python
import functools
import math

import jax
import jax.numpy as jnp
from jax import lax
from jax.experimental import pallas as pl
from jax.experimental.pallas import tpu as pltpu
from jax.sharding import PartitionSpec as P

MESH = pl.DeviceIdType.MESH
F32 = jnp.float32
BF16 = jnp.bfloat16
NEV, NS, COLORS, LS, NSRC, NT, SPACE = 128, 4, 3, 96, 128, 16, 8
SITES_TOTAL = 4096
SITES = SITES_TOTAL // SPACE
SLICE = NEV // SPACE
ROWS_X, ROWS_Y, ROWS_Z = pl.ds(0, 32), pl.ds(32, 32), pl.ds(64, 64)
SHIFTS = (1, -1, 2)


def site_phases(mom_ref, space):
    site = (space * SITES + lax.broadcasted_iota(jnp.int32, (1, SITES), 1)).astype(F32)
    line = jnp.floor((site + 0.5) * (1.0 / LS))
    coord_x = site - LS * line
    coord_z = jnp.floor((line + 0.5) * (1.0 / LS))
    coord_y = line - LS * coord_z
    m = [mom_ref[0, i].astype(F32) for i in range(3)]
    turns = m[0] * coord_x + m[1] * coord_y + m[2] * coord_z
    turns = turns - LS * jnp.floor((turns + 0.5) * (1.0 / LS))
    angle = (2.0 * math.pi / LS) * turns
    return jnp.cos(angle), -jnp.sin(angle)


def kernel(
    mom_ref, gam_ref, eig_hbm, fwd_hbm, back_hbm, out_ref,
    eig, fbuf, bbuf, part, rs, ebuf, gbuf, fin, finr,
    load_sem, swap_sem, rs_send, rs_recv, e_send, e_recv, f_send, f_recv, fin_sem,
):
    t = lax.axis_index("tins")
    space = lax.axis_index("space")
    core = lax.rem(t, 2)
    x, y_hi = lax.div(t, 4), lax.rem(lax.div(t, 2), 2)
    z, y_lo = lax.div(space, 2), lax.rem(space, 2)
    k_own = lax.div(t, 2)
    partner = (t + 1 - 2 * core, space)

    def step(v, d):
        return lax.rem(v + (d + 4) % 4, 4) if d % 4 else v

    def chip(dx, flip_hi, dz, flip_lo):
        hi = 1 - y_hi if flip_hi else y_hi
        lo = 1 - y_lo if flip_lo else y_lo
        return (step(x, dx) * 4 + hi * 2 + core, step(z, dz) * 2 + lo)

    PAIR, ACROSS, TWO = (False, True), (True, True), (True, False)

    loads = [pltpu.make_async_copy(eig_hbm.at[:, c], eig.at[:, c], load_sem.at[c]) for c in range(COLORS)]
    loads += [
        pltpu.make_async_copy(fwd_hbm, fbuf.at[x, y_hi], load_sem.at[3]),
        pltpu.make_async_copy(back_hbm.at[:, core], bbuf.at[:, core], load_sem.at[4]),
    ]
    for load in loads:
        load.start()

    barrier = pltpu.get_barrier_semaphore()
    peers = [partner]
    peers += [(t, lax.rem(space + d, SPACE)) for d in range(1, SPACE)]
    peers += [chip(d, False, 0, False) for d in SHIFTS]
    peers += [chip(d, True, 0, True) for d in (0, *SHIFTS)]
    peers += [chip(0, True, 0, False)]
    for peer in peers:
        pl.semaphore_signal(barrier, inc=1, device_id=peer, device_id_type=MESH)

    phase_re, phase_im = site_phases(mom_ref, space)
    total = jnp.zeros((NEV, 2 * NEV), F32)
    nt = (((1,), (1,)), ((), ()))
    for color in range(COLORS):
        loads[color].wait()
        vec_re = eig[0, color]
        vec_im = eig[1, color]
        wide_re, wide_im = vec_re.astype(F32), vec_im.astype(F32)
        wave_re = (phase_re * wide_re - phase_im * wide_im).astype(BF16)
        wave_im = (phase_re * wide_im + phase_im * wide_re).astype(BF16)
        right = jnp.concatenate([wave_re, wave_im], axis=0)
        total += lax.dot_general(vec_re, right, nt, preferred_element_type=F32)
        right = jnp.concatenate([wave_im, -wave_re], axis=0)
        total += lax.dot_general(vec_im, right, nt, preferred_element_type=F32)
    part[...] = total.reshape(SPACE, SLICE, 2 * NEV)

    loads[3].wait()
    pl.semaphore_wait(barrier, len(peers))
    copies = []

    def send(src, dst, send_sem, recv_sem, device):
        copy = pltpu.make_async_remote_copy(
            src_ref=src, dst_ref=dst, send_sem=send_sem, recv_sem=recv_sem,
            device_id=device, device_id_type=MESH,
        )
        copy.start()
        copies.append(copy)
        return copy

    scatter = []
    for d in range(1, SPACE):
        to = lax.rem(space + d, SPACE)
        scatter.append(send(part.at[to], rs.at[d], rs_send.at[d], rs_recv.at[d], (t, to)))

    got = {}

    def share(name, block, device):
        n = len(got)
        got[name] = send(block, block, f_send.at[n], f_recv.at[n], device)

    def z_block(dx, flip):
        hi = 1 - y_hi if flip else y_hi
        return fbuf.at[step(x, dx), hi, z, :, ROWS_Z]

    def y_block(dx):
        return fbuf.at[step(x, dx), y_hi, :, y_lo, ROWS_Y]

    def x_block(flip):
        hi = 1 - y_hi if flip else y_hi
        return fbuf.at[x, hi, :, :, ROWS_X]

    for d in (2, 1, -1):
        share(("z1", d, True), z_block(0, False), chip(d, True, 0, True))
        share(("z1", d, False), z_block(0, False), chip(d, False, 0, False))
        share(("y1", d), y_block(0), chip(d, False, 0, False))
    share(("z1", 0, True), z_block(0, False), chip(0, True, 0, True))
    share(("x1",), x_block(False), chip(0, True, 0, True))
    for d in SHIFTS:
        share(("x2", d, False), x_block(False), chip(d, False, 0, False))
    for name, flips in (("across", ACROSS), ("two", TWO)):
        share(("y2", name, 0), y_block(0), chip(0, flips[0], 0, flips[1]))
    swap = send(
        back_hbm.at[:, 1 - core], bbuf.at[:, core], swap_sem.at[0], swap_sem.at[1], partner
    )

    elem = part[space]
    for d in range(1, SPACE):
        scatter[d - 1].wait_recv()
        elem += rs[d]
    own = k_own * SPACE + space
    ebuf[own] = (elem * (1.0 / math.sqrt(3.0 * SITES_TOTAL))).astype(BF16)
    away = [
        (dx, flip_hi, dz, flip_lo)
        for dx in (0, *SHIFTS) for flip_hi in (False, True)
        for dz in (0, *SHIFTS) for flip_lo in (False, True)
    ]
    def hops(at):
        dx, flip_hi, dz, flip_lo = at
        return abs(dx) + abs(dz) + (1 if flip_lo else 2 * flip_hi)
    for at in sorted(away[1:], key=hops, reverse=True):
        pltpu.make_async_remote_copy(
            src_ref=ebuf.at[own], dst_ref=ebuf.at[own], send_sem=e_send.at[0],
            recv_sem=e_recv.at[k_own], device_id=chip(*at), device_id_type=MESH,
        ).start()

    got["x1",].wait_recv()
    for d in SHIFTS:
        share(("x2", d, True), x_block(True), chip(d, False, 0, False))
    for d in SHIFTS:
        got["y1", d].wait_recv()
        for name, flips in (("two", TWO), ("across", ACROSS), ("pair", PAIR)):
            share(("y2", name, d), y_block(-d), chip(0, flips[0], 0, flips[1]))
    for dx, flip in [(0, True)] + [(d, f) for d in SHIFTS for f in (False, True)]:
        got["z1", dx, flip].wait_recv()
        for d in (2, 1, -1):
            share(("z2", dx, flip, d), z_block(-dx, flip), chip(0, False, d, False))

    loads[4].wait()
    swap.wait_recv()
    for spin in range(NS):
        power = gam_ref[1, spin]
        cosine = jnp.where(power == 0, 1.0, 0.0) - jnp.where(power == 2, 1.0, 0.0)
        sine = jnp.where(power == 1, 1.0, 0.0) - jnp.where(power == 3, 1.0, 0.0)
        lanes = pl.ds(spin * NEV, NEV)

        def turn(k, carry):
            for u in range(2):
                back_re = bbuf[k, u, 0:64, lanes].astype(F32)
                back_im = bbuf[k, u, 64:128, lanes].astype(F32)
                bbuf[k, u, 0:64, lanes] = (cosine * back_re - sine * back_im).astype(BF16)
                bbuf[k, u, 64:128, lanes] = (sine * back_re + cosine * back_im).astype(BF16)
            return carry

        lax.fori_loop(0, NT // 2, turn, 0)

    acc = jnp.zeros((4 * 64, 2 * NSRC), F32)
    for dx in (0, *SHIFTS):
        for flip in (False, True):
            x_at, hi_at = step(x, -dx), 1 - y_hi if flip else y_hi
            k = x_at * 2 + hi_at
            here = dx == 0 and not flip
            rows = pl.ds(k * SPACE, SPACE)
            count = pl.ds(0, SPACE - 1) if here else pl.ds(0, SPACE)
            pltpu.make_async_copy(ebuf.at[count], ebuf.at[count], e_recv.at[k]).wait()
            if not here:
                if dx:
                    got["x2", dx, flip].wait_recv()
                if flip:
                    got["y2", "across", dx].wait_recv()
                    got["y2", "two", dx].wait_recv()
                else:
                    got["y2", "pair", dx].wait_recv()
                for d in SHIFTS:
                    got["z2", dx, flip, d].wait_recv()
            elem = ebuf[rows].reshape(NEV, 2 * NEV)
            for spin in range(NS):
                fwd_re = fbuf[x_at, hi_at, spin // 2, spin % 2]
                fwd_im = fbuf[x_at, hi_at, 2 + spin // 2, spin % 2]
                right = jnp.concatenate([
                    jnp.concatenate([fwd_re, fwd_im], axis=1),
                    jnp.concatenate([-fwd_im, fwd_re], axis=1),
                ], axis=0)
                gbuf[spin] = jnp.dot(elem, right, preferred_element_type=F32).astype(BF16)
            image = jnp.concatenate([gbuf[gam_ref[0, spin]] for spin in range(NS)], axis=0)
            left = bbuf[k].reshape(4 * 64, NS * NEV)
            acc += jnp.dot(left, image, preferred_element_type=F32)
    for u in range(2):
        top = acc[u * 128 : u * 128 + 64]
        low = acc[u * 128 + 64 : u * 128 + 128]
        fin[u, 0] = top[:, :NSRC] - low[:, NSRC:]
        fin[u, 1] = top[:, NSRC:] + low[:, :NSRC]
    last = send(fin.at[1 - core], finr, fin_sem.at[0], fin_sem.at[1], partner)
    last.wait_recv()
    out_ref[...] = (fin[core] + finr[...]) * (1.0 / math.sqrt(NT))
    for copy in copies:
        copy.wait_send()
    sent = pl.ds(0, 63)
    pltpu.make_async_copy(ebuf.at[sent], ebuf.at[sent], e_send.at[0]).wait()


def on_device(eigvecs, momenta, gamma_table, forward, backward):
    eig = eigvecs[0].transpose(0, 2, 1, 3)
    fwd = forward.reshape(4, 2, NEV, NSRC)
    back = backward.reshape(NT // 2, 2, 128, NS * NEV)
    dma = pltpu.SemaphoreType.DMA
    out = pl.pallas_call(
        kernel,
        name="three_point",
        out_shape=jax.ShapeDtypeStruct((2, 64, NSRC), F32),
        in_specs=[pl.BlockSpec(memory_space=pltpu.SMEM)] * 2
        + [pl.BlockSpec(memory_space=pl.ANY)] * 3,
        out_specs=pl.BlockSpec(memory_space=pltpu.VMEM),
        scratch_shapes=[
            pltpu.VMEM((2, COLORS, NEV, SITES), BF16),
            pltpu.VMEM((4, 2, 4, 2, NEV, NSRC), BF16),
            pltpu.VMEM((NT // 2, 2, 128, NS * NEV), BF16),
            pltpu.VMEM((SPACE, SLICE, 2 * NEV), F32),
            pltpu.VMEM((SPACE, SLICE, 2 * NEV), F32),
            pltpu.VMEM((64, SLICE, 2 * NEV), BF16),
            pltpu.VMEM((NS, NEV, 2 * NSRC), BF16),
            pltpu.VMEM((2, 2, 64, NSRC), F32),
            pltpu.VMEM((2, 64, NSRC), F32),
            dma((5,)), dma((2,)), dma((SPACE,)), dma((SPACE,)),
            dma((1,)), dma((8,)), dma((49,)), dma((49,)), dma((2,)),
        ],
        compiler_params=pltpu.CompilerParams(collective_id=0, has_side_effects=True),
    )(momenta, gamma_table, eig, fwd, back)
    return out[None, None]


def solution(mesh):
    placed = (
        P("tins", None, None, None, "space"),
        P(),
        P(),
        P("tins", None, None, None),
        P("tins", None, None, "space", None),
    )
    return jax.shard_map(
        on_device,
        mesh=mesh,
        in_specs=placed,
        out_specs=P("tins", None, None, "space", None),
        check_vma=False,
    )
```

time: 38.5 us -> 37.5 us (0.974)
  Pallas kernels: 36.8 us -> 35.8 us
    pallas_call x1, Pallas kernels: 36.8 us -> 35.8 us  [on_device(): pl.pallas_call(kernel, name='three_point', out_shape=jax.ShapeDtypeStruct...]
where the time goes in v2:
time: 37.5 us; the launch traced here: 37.3 us
  Pallas kernels  35.8 us (95%)
  local copies, waits for them, and re-layouts  1.47 us (4%)
    pallas_call x1, Pallas kernels, on_device(): pl.pallas_call(kernel, name='three_point', out_shape=jax.ShapeDtypeStruct...  35.8 us
    unnamed x1, local copies, waits for them, and re-layouts  1.47 us

profile of v2, /device:TPU:1, one launch (start us, length us, event | category | flops | bytes accessed | tf_op | source)
XLA Modules:
  0.0 37.3 jit_solution(16174133809220658598)
XLA Ops:
  0.0 35.8 %three_point.1 = f32[2,64,128]{2,1,0:T(8,128)} custom-call(s32[1,3]{1,0:T(1,128)} %mom_ref.1, s32[2,4]{1,0:T(2,128)} %gam_ref.1, bf16[2,3,128,512]{3,2,1,0:T(8,128)(2,1)} %bitcast.7, bf16[4,2,128,128]{3,2,1,0:T(8,128)(2,1)} %bitcast.8, bf16[8,2,128,512]{3,2,1,0:T(8,128)(2,1)} %bitcast.6), custom_call_target="tpu_custom_call" | custom-call | tf_op jit(solution)/shard_map/three_point/pallas_call | solution.py:240
  35.8 1.5 %copy.7 = f32[1,1,2,64,128]{4,3,2,1,0:T(8,128)} copy(f32[1,1,2,64,128]{4,3,2,1,0:T(8,128)} %bitcast.9) | data formatting | bytes 131072

commit v3 on v2

--- a/solution.py
+++ b/solution.py
@@ -15,7 +15,7 @@
 SITES_TOTAL = 4096
 SITES = SITES_TOTAL // SPACE
 SLICE = NEV // SPACE
-ROWS_X, ROWS_Y, ROWS_Z = pl.ds(0, 32), pl.ds(32, 32), pl.ds(64, 64)
+ROWS_X, ROWS_Y, ROWS_Z = pl.ds(0, 48), pl.ds(48, 48), pl.ds(96, 32)
 SHIFTS = (1, -1, 2)
 
 
@@ -225,7 +225,7 @@
         fin[u, 1] = top[:, NSRC:] + low[:, :NSRC]
     last = send(fin.at[1 - core], finr, fin_sem.at[0], fin_sem.at[1], partner)
     last.wait_recv()
-    out_ref[...] = (fin[core] + finr[...]) * (1.0 / math.sqrt(NT))
+    out_ref[...] = fin[core] + finr[...]
     for copy in copies:
         copy.wait_send()
     sent = pl.ds(0, 63)
@@ -240,7 +240,7 @@
     out = pl.pallas_call(
         kernel,
         name="three_point",
-        out_shape=jax.ShapeDtypeStruct((2, 64, NSRC), F32),
+        out_shape=pltpu.VMEM((2, 64, NSRC), F32),
         in_specs=[pl.BlockSpec(memory_space=pltpu.SMEM)] * 2
         + [pl.BlockSpec(memory_space=pl.ANY)] * 3,
         out_specs=pl.BlockSpec(memory_space=pltpu.VMEM),
@@ -259,7 +259,7 @@
         ],
         compiler_params=pltpu.CompilerParams(collective_id=0, has_side_effects=True),
     )(momenta, gamma_table, eig, fwd, back)
-    return out[None, None]
+    return out[None, None] * (1.0 / math.sqrt(NT))
 
 
 def solution(mesh):

time: 37.5 us -> 32 us (0.85)
  Pallas kernels: 35.8 us -> 31.2 us
  local copies, waits for them, and re-layouts: 1.47 us -> 0 us
  other arithmetic: 0 us -> 0.64 us
    pallas_call x1, Pallas kernels: 35.8 us -> 31.2 us  [on_device(): pl.pallas_call(kernel, name='three_point', out_shape=pltpu.VMEM((2, 64, N...]
    unnamed x1 -> x0, local copies, waits for them, and re-layouts: 1.47 us -> none
    mul x0 -> x1, other arithmetic: none -> 0.64 us  [on_device(): return out[None, None] * (1.0 / math.sqrt(NT))]
where the time goes in v3:
time: 32 us; the launch traced here: 31.9 us
  Pallas kernels  31.2 us (98%)
  other arithmetic  0.64 us (2%)
    pallas_call x1, Pallas kernels, on_device(): pl.pallas_call(kernel, name='three_point', out_shape=pltpu.VMEM((2, 64, N...  31.2 us

profile of v3, /device:TPU:1, one launch (start us, length us, event | category | flops | bytes accessed | tf_op | source)
XLA Modules:
  0.0 31.9 jit_solution(218991777092017884)
XLA Ops:
  0.0 31.2 %three_point.1 = f32[2,64,128]{2,1,0:T(8,128)S(1)} custom-call(s32[1,3]{1,0:T(1,128)} %mom_ref.1, s32[2,4]{1,0:T(2,128)} %gam_ref.1, bf16[2,3,128,512]{3,2,1,0:T(8,128)(2,1)} %bitcast.8, bf16[4,2,128,128]{3,2,1,0:T(8,128)(2,1)} %bitcast.9, bf16[8,2,128,512]{3,2,1,0:T(8,128)(2,1)} %bitcast.7), custom_call_target="tpu_custom_call" | custom-call | tf_op jit(solution)/shard_map/three_point/pallas_call | solution.py:240
  31.2 0.6 %multiply_bitcast_fusion = f32[1,1,2,64,128]{4,3,2,1,0:T(8,128)} fusion(f32[2,64,128]{2,1,0:T(8,128)S(1)} %three_point.1), kind=kLoop, calls=%fused_computation | loop fusion | flops 16384 | bytes 131072 | tf_op jit(solution)/shard_map/mul | solution.py:262

commit v4 on v3

--- a/solution.py
+++ b/solution.py
@@ -15,7 +15,7 @@
 SITES_TOTAL = 4096
 SITES = SITES_TOTAL // SPACE
 SLICE = NEV // SPACE
-ROWS_X, ROWS_Y, ROWS_Z = pl.ds(0, 48), pl.ds(48, 48), pl.ds(96, 32)
+ROWS_X, ROWS_Y, ROWS_Z = pl.ds(0, 48), pl.ds(48, 64), pl.ds(112, 16)
 SHIFTS = (1, -1, 2)
 
 
@@ -35,7 +35,7 @@
 def kernel(
     mom_ref, gam_ref, eig_hbm, fwd_hbm, back_hbm, out_ref,
     eig, fbuf, bbuf, part, rs, ebuf, gbuf, fin, finr,
-    load_sem, swap_sem, rs_send, rs_recv, e_send, e_recv, f_send, f_recv, fin_sem,
+    load_sem, swap_sem, rs_send, rs_recv, e_send, e_recv, e2_send, e2_recv, f_send, f_recv, fin_sem,
 ):
     t = lax.axis_index("tins")
     space = lax.axis_index("space")
@@ -109,7 +109,7 @@
     got = {}
 
     def share(name, block, device):
-        n = len(got)
+        n = sum(key[0] != "e2" for key in got)
         got[name] = send(block, block, f_send.at[n], f_recv.at[n], device)
 
     def z_block(dx, flip):
@@ -129,10 +129,7 @@
         share(("y1", d), y_block(0), chip(d, False, 0, False))
     share(("z1", 0, True), z_block(0, False), chip(0, True, 0, True))
     share(("x1",), x_block(False), chip(0, True, 0, True))
-    for d in SHIFTS:
-        share(("x2", d, False), x_block(False), chip(d, False, 0, False))
-    for name, flips in (("across", ACROSS), ("two", TWO)):
-        share(("y2", name, 0), y_block(0), chip(0, flips[0], 0, flips[1]))
+    share(("y2", "across", 0), y_block(0), chip(0, True, 0, True))
     swap = send(
         back_hbm.at[:, 1 - core], bbuf.at[:, core], swap_sem.at[0], swap_sem.at[1], partner
     )
@@ -141,33 +138,42 @@
     for d in range(1, SPACE):
         scatter[d - 1].wait_recv()
         elem += rs[d]
-    own = k_own * SPACE + space
-    ebuf[own] = (elem * (1.0 / math.sqrt(3.0 * SITES_TOTAL))).astype(BF16)
-    away = [
-        (dx, flip_hi, dz, flip_lo)
-        for dx in (0, *SHIFTS) for flip_hi in (False, True)
-        for dz in (0, *SHIFTS) for flip_lo in (False, True)
-    ]
-    def hops(at):
-        dx, flip_hi, dz, flip_lo = at
-        return abs(dx) + abs(dz) + (1 if flip_lo else 2 * flip_hi)
-    for at in sorted(away[1:], key=hops, reverse=True):
-        pltpu.make_async_remote_copy(
-            src_ref=ebuf.at[own], dst_ref=ebuf.at[own], send_sem=e_send.at[0],
-            recv_sem=e_recv.at[k_own], device_id=chip(*at), device_id_type=MESH,
-        ).start()
-
+    ebuf[k_own, space] = (elem * (1.0 / math.sqrt(3.0 * SITES_TOTAL))).astype(BF16)
+    own = ebuf.at[k_own, space]
+    for dx in (2, 1, -1, 0):
+        for flips in (TWO, ACROSS, PAIR, (False, False)):
+            if dx or flips[0] or flips[1]:
+                pltpu.make_async_remote_copy(
+                    src_ref=own, dst_ref=own, send_sem=e_send.at[0], recv_sem=e_recv.at[x],
+                    device_id=chip(dx, flips[0], 0, flips[1]), device_id_type=MESH,
+                ).start()
+
+    for d in SHIFTS:
+        share(("x2", d, False), x_block(False), chip(d, False, 0, False))
     got["x1",].wait_recv()
     for d in SHIFTS:
         share(("x2", d, True), x_block(True), chip(d, False, 0, False))
     for d in SHIFTS:
         got["y1", d].wait_recv()
-        for name, flips in (("two", TWO), ("across", ACROSS), ("pair", PAIR)):
+        for name, flips in (("across", ACROSS), ("pair", PAIR)):
             share(("y2", name, d), y_block(-d), chip(0, flips[0], 0, flips[1]))
     for dx, flip in [(0, True)] + [(d, f) for d in SHIFTS for f in (False, True)]:
         got["z1", dx, flip].wait_recv()
         for d in (2, 1, -1):
             share(("z2", dx, flip, d), z_block(-dx, flip), chip(0, False, d, False))
+    for i, dx in enumerate((0, *SHIFTS)):
+        x_at = step(x, -dx)
+        fill = ebuf.at[0, pl.ds(0, 3)] if dx == 0 else ebuf.at[pl.ds(0, 2), pl.ds(0, 2)]
+        pltpu.make_async_copy(fill, fill, e_recv.at[x_at]).wait()
+        four = ebuf.at[pl.ds(2 * x_at, 2), pl.ds(2 * z, 2)]
+        for d in (2, 1, -1):
+            got["e2", dx, d] = send(
+                four, four, e2_send.at[i, d + 1], e2_recv.at[i, d + 1], chip(0, False, d, False)
+            )
+    for d in (0, *SHIFTS):
+        got["y2", "across", d].wait_recv()
+        passed = fbuf.at[step(x, -d), 1 - y_hi, :, 1 - y_lo, ROWS_Y]
+        share(("y3", d), passed, chip(0, False, 0, True))
 
     loads[4].wait()
     swap.wait_recv()
@@ -193,20 +199,19 @@
             x_at, hi_at = step(x, -dx), 1 - y_hi if flip else y_hi
             k = x_at * 2 + hi_at
             here = dx == 0 and not flip
-            rows = pl.ds(k * SPACE, SPACE)
-            count = pl.ds(0, SPACE - 1) if here else pl.ds(0, SPACE)
-            pltpu.make_async_copy(ebuf.at[count], ebuf.at[count], e_recv.at[k]).wait()
+            if not flip:
+                for d in SHIFTS:
+                    got["e2", dx, d].wait_recv()
             if not here:
                 if dx:
                     got["x2", dx, flip].wait_recv()
                 if flip:
-                    got["y2", "across", dx].wait_recv()
-                    got["y2", "two", dx].wait_recv()
+                    got["y3", dx].wait_recv()
                 else:
                     got["y2", "pair", dx].wait_recv()
                 for d in SHIFTS:
                     got["z2", dx, flip, d].wait_recv()
-            elem = ebuf[rows].reshape(NEV, 2 * NEV)
+            elem = ebuf[k].reshape(NEV, 2 * NEV)
             for spin in range(NS):
                 fwd_re = fbuf[x_at, hi_at, spin // 2, spin % 2]
                 fwd_im = fbuf[x_at, hi_at, 2 + spin // 2, spin % 2]
@@ -228,8 +233,8 @@
     out_ref[...] = fin[core] + finr[...]
     for copy in copies:
         copy.wait_send()
-    sent = pl.ds(0, 63)
-    pltpu.make_async_copy(ebuf.at[sent], ebuf.at[sent], e_send.at[0]).wait()
+    sent = ebuf.at[pl.ds(0, 3), pl.ds(0, 5)]
+    pltpu.make_async_copy(sent, sent, e_send.at[0]).wait()
 
 
 def on_device(eigvecs, momenta, gamma_table, forward, backward):
@@ -250,12 +255,12 @@
             pltpu.VMEM((NT // 2, 2, 128, NS * NEV), BF16),
             pltpu.VMEM((SPACE, SLICE, 2 * NEV), F32),
             pltpu.VMEM((SPACE, SLICE, 2 * NEV), F32),
-            pltpu.VMEM((64, SLICE, 2 * NEV), BF16),
+            pltpu.VMEM((NT // 2, SPACE, SLICE, 2 * NEV), BF16),
             pltpu.VMEM((NS, NEV, 2 * NSRC), BF16),
             pltpu.VMEM((2, 2, 64, NSRC), F32),
             pltpu.VMEM((2, 64, NSRC), F32),
             dma((5,)), dma((2,)), dma((SPACE,)), dma((SPACE,)),
-            dma((1,)), dma((8,)), dma((49,)), dma((49,)), dma((2,)),
+            dma((1,)), dma((4,)), dma((4, 4)), dma((4, 4)), dma((49,)), dma((49,)), dma((2,)),
         ],
         compiler_params=pltpu.CompilerParams(collective_id=0, has_side_effects=True),
     )(momenta, gamma_table, eig, fwd, back)

time: 32 us -> 30.5 us (0.953)
  Pallas kernels: 31.2 us -> 29.7 us
    pallas_call x1, Pallas kernels: 31.2 us -> 29.7 us  [on_device(): pl.pallas_call(kernel, name='three_point', out_shape=pltpu.VMEM((2, 64, N...]
where the time goes in v4:
time: 30.5 us; the launch traced here: 30.4 us
  Pallas kernels  29.7 us (97%)
  other arithmetic  0.64 us (2%)
    pallas_call x1, Pallas kernels, on_device(): pl.pallas_call(kernel, name='three_point', out_shape=pltpu.VMEM((2, 64, N...  29.7 us
    mul x1, other arithmetic, on_device(): return out[None, None] * (1.0 / math.sqrt(NT))  0.64 us

profile of v4, /device:TPU:1, one launch (start us, length us, event | category | flops | bytes accessed | tf_op | source)
XLA Modules:
  0.0 30.4 jit_solution(6069624325922538442)
XLA Ops:
  0.0 29.7 %three_point.1 = f32[2,64,128]{2,1,0:T(8,128)S(1)} custom-call(s32[1,3]{1,0:T(1,128)} %mom_ref.1, s32[2,4]{1,0:T(2,128)} %gam_ref.1, bf16[2,3,128,512]{3,2,1,0:T(8,128)(2,1)} %bitcast.8, bf16[4,2,128,128]{3,2,1,0:T(8,128)(2,1)} %bitcast.9, bf16[8,2,128,512]{3,2,1,0:T(8,128)(2,1)} %bitcast.7), custom_call_target="tpu_custom_call" | custom-call | tf_op jit(solution)/shard_map/three_point/pallas_call | solution.py:245
  29.7 0.6 %multiply_bitcast_fusion = f32[1,1,2,64,128]{4,3,2,1,0:T(8,128)} fusion(f32[2,64,128]{2,1,0:T(8,128)S(1)} %three_point.1), kind=kLoop, calls=%fused_computation | loop fusion | flops 16384 | bytes 131072 | tf_op jit(solution)/shard_map/mul | solution.py:267

commit v5 on v4

--- a/solution.py
+++ b/solution.py
@@ -55,6 +55,17 @@
 
     PAIR, ACROSS, TWO = (False, True), (True, True), (True, False)
 
+    barrier = pltpu.get_barrier_semaphore()
+    shared = [(2, True), (2, False), (1, True), (-1, True), (1, False), (-1, False), (0, True)]
+    peers = [chip(0, False, *at) for at in shared[:4]]
+    peers += [chip(d, True, 0, True) for d in (2, 1, -1)]
+    peers += [chip(0, False, *at) for at in shared[4:6]]
+    peers += [chip(d, False, 0, False) for d in (2, 1, -1)]
+    peers += [chip(0, *flips) for flips in ((True, 0, False), (True, 0, True), (False, 0, True))]
+    peers += [partner]
+    for peer in peers:
+        pl.semaphore_signal(barrier, inc=1, device_id=peer, device_id_type=MESH)
+
     loads = [pltpu.make_async_copy(eig_hbm.at[:, c], eig.at[:, c], load_sem.at[c]) for c in range(COLORS)]
     loads += [
         pltpu.make_async_copy(fwd_hbm, fbuf.at[x, y_hi], load_sem.at[3]),
@@ -62,15 +73,6 @@
     ]
     for load in loads:
         load.start()
-
-    barrier = pltpu.get_barrier_semaphore()
-    peers = [partner]
-    peers += [(t, lax.rem(space + d, SPACE)) for d in range(1, SPACE)]
-    peers += [chip(d, False, 0, False) for d in SHIFTS]
-    peers += [chip(d, True, 0, True) for d in (0, *SHIFTS)]
-    peers += [chip(0, True, 0, False)]
-    for peer in peers:
-        pl.semaphore_signal(barrier, inc=1, device_id=peer, device_id_type=MESH)
 
     phase_re, phase_im = site_phases(mom_ref, space)
     total = jnp.zeros((NEV, 2 * NEV), F32)
@@ -102,9 +104,9 @@
         return copy
 
     scatter = []
-    for d in range(1, SPACE):
-        to = lax.rem(space + d, SPACE)
-        scatter.append(send(part.at[to], rs.at[d], rs_send.at[d], rs_recv.at[d], (t, to)))
+    for d, at in enumerate(shared):
+        to = chip(0, False, *at)
+        scatter.append(send(part.at[to[1]], rs.at[d], rs_send.at[d], rs_recv.at[d], to))
 
     got = {}
 
@@ -130,13 +132,15 @@
     share(("z1", 0, True), z_block(0, False), chip(0, True, 0, True))
     share(("x1",), x_block(False), chip(0, True, 0, True))
     share(("y2", "across", 0), y_block(0), chip(0, True, 0, True))
+    for d in (1, -1):
+        share(("x2", d, False), x_block(False), chip(d, False, 0, False))
     swap = send(
         back_hbm.at[:, 1 - core], bbuf.at[:, core], swap_sem.at[0], swap_sem.at[1], partner
     )
 
     elem = part[space]
-    for d in range(1, SPACE):
-        scatter[d - 1].wait_recv()
+    for d in range(len(shared)):
+        scatter[d].wait_recv()
         elem += rs[d]
     ebuf[k_own, space] = (elem * (1.0 / math.sqrt(3.0 * SITES_TOTAL))).astype(BF16)
     own = ebuf.at[k_own, space]
@@ -148,7 +152,7 @@
                     device_id=chip(dx, flips[0], 0, flips[1]), device_id_type=MESH,
                 ).start()
 
-    for d in SHIFTS:
+    for d in (2,):
         share(("x2", d, False), x_block(False), chip(d, False, 0, False))
     got["x1",].wait_recv()
     for d in SHIFTS:
@@ -166,7 +170,7 @@
         fill = ebuf.at[0, pl.ds(0, 3)] if dx == 0 else ebuf.at[pl.ds(0, 2), pl.ds(0, 2)]
         pltpu.make_async_copy(fill, fill, e_recv.at[x_at]).wait()
         four = ebuf.at[pl.ds(2 * x_at, 2), pl.ds(2 * z, 2)]
-        for d in (2, 1, -1):
+        for d in SHIFTS:
             got["e2", dx, d] = send(
                 four, four, e2_send.at[i, d + 1], e2_recv.at[i, d + 1], chip(0, False, d, False)
             )

time: 30.5 us -> 30.2 us (level)
    pallas_call x1, Pallas kernels: 29.7 us -> 29.4 us  [on_device(): pl.pallas_call(kernel, name='three_point', out_shape=pltpu.VMEM((2, 64, N...]
where the time goes in v5:
time: 30.2 us; the launch traced here: 30.1 us
  Pallas kernels  29.4 us (97%)
  other arithmetic  0.64 us (2%)
    pallas_call x1, Pallas kernels, on_device(): pl.pallas_call(kernel, name='three_point', out_shape=pltpu.VMEM((2, 64, N...  29.4 us
    mul x1, other arithmetic, on_device(): return out[None, None] * (1.0 / math.sqrt(NT))  0.64 us

profile of v5, /device:TPU:1, one launch (start us, length us, event | category | flops | bytes accessed | tf_op | source)
XLA Modules:
  0.0 30.1 jit_solution(14433239586595626322)
XLA Ops:
  0.0 29.4 %three_point.1 = f32[2,64,128]{2,1,0:T(8,128)S(1)} custom-call(s32[1,3]{1,0:T(1,128)} %mom_ref.1, s32[2,4]{1,0:T(2,128)} %gam_ref.1, bf16[2,3,128,512]{3,2,1,0:T(8,128)(2,1)} %bitcast.8, bf16[4,2,128,128]{3,2,1,0:T(8,128)(2,1)} %bitcast.9, bf16[8,2,128,512]{3,2,1,0:T(8,128)(2,1)} %bitcast.7), custom_call_target="tpu_custom_call" | custom-call | tf_op jit(solution)/shard_map/three_point/pallas_call | solution.py:249
  29.4 0.6 %multiply_bitcast_fusion = f32[1,1,2,64,128]{4,3,2,1,0:T(8,128)} fusion(f32[2,64,128]{2,1,0:T(8,128)S(1)} %three_point.1), kind=kLoop, calls=%fused_computation | loop fusion | flops 16384 | bytes 131072 | tf_op jit(solution)/shard_map/mul | solution.py:271

commit v6 on v5

--- a/solution.py
+++ b/solution.py
@@ -131,7 +131,6 @@
         share(("y1", d), y_block(0), chip(d, False, 0, False))
     share(("z1", 0, True), z_block(0, False), chip(0, True, 0, True))
     share(("x1",), x_block(False), chip(0, True, 0, True))
-    share(("y2", "across", 0), y_block(0), chip(0, True, 0, True))
     for d in (1, -1):
         share(("x2", d, False), x_block(False), chip(d, False, 0, False))
     swap = send(
@@ -152,11 +151,12 @@
                     device_id=chip(dx, flips[0], 0, flips[1]), device_id_type=MESH,
                 ).start()
 
-    for d in (2,):
-        share(("x2", d, False), x_block(False), chip(d, False, 0, False))
+    share(("y2", "across", 0), y_block(0), chip(0, True, 0, True))
     got["x1",].wait_recv()
     for d in SHIFTS:
         share(("x2", d, True), x_block(True), chip(d, False, 0, False))
+    for d in (2,):
+        share(("x2", d, False), x_block(False), chip(d, False, 0, False))
     for d in SHIFTS:
         got["y1", d].wait_recv()
         for name, flips in (("across", ACROSS), ("pair", PAIR)):

time: 30.2 us -> 30.2 us (level)
  no operation moved by 1% of the time
where the time goes in v6:
time: 30.2 us; the launch traced here: 30 us
  Pallas kernels  29.4 us (97%)
  other arithmetic  0.64 us (2%)
    pallas_call x1, Pallas kernels, on_device(): pl.pallas_call(kernel, name='three_point', out_shape=pltpu.VMEM((2, 64, N...  29.4 us
    mul x1, other arithmetic, on_device(): return out[None, None] * (1.0 / math.sqrt(NT))  0.64 us

profile of v6, /device:TPU:1, one launch (start us, length us, event | category | flops | bytes accessed | tf_op | source)
XLA Modules:
  0.0 30.0 jit_solution(14084809205022591620)
XLA Ops:
  0.0 29.4 %three_point.1 = f32[2,64,128]{2,1,0:T(8,128)S(1)} custom-call(s32[1,3]{1,0:T(1,128)} %mom_ref.1, s32[2,4]{1,0:T(2,128)} %gam_ref.1, bf16[2,3,128,512]{3,2,1,0:T(8,128)(2,1)} %bitcast.8, bf16[4,2,128,128]{3,2,1,0:T(8,128)(2,1)} %bitcast.9, bf16[8,2,128,512]{3,2,1,0:T(8,128)(2,1)} %bitcast.7), custom_call_target="tpu_custom_call" | custom-call | tf_op jit(solution)/shard_map/three_point/pallas_call | solution.py:249
  29.4 0.6 %multiply_bitcast_fusion = f32[1,1,2,64,128]{4,3,2,1,0:T(8,128)} fusion(f32[2,64,128]{2,1,0:T(8,128)S(1)} %three_point.1), kind=kLoop, calls=%fused_computation | loop fusion | flops 16384 | bytes 131072 | tf_op jit(solution)/shard_map/mul | solution.py:271
